TPU v7x, 32 devices: a whole 2x2x4 slice. The times are simulated.
32 devices in a mesh: ens: 2 (over x), lat: 4 (over y, core), lon: 4 (over z).
Axes of the slice: x: 2, y: 2, z: 4, core: 2. Of those that a mesh axis runs over, the one named last changes fastest.
Arguments:
- starting_state: bfloat16 [4, 222, 128, 512], P('ens', None, 'lat', 'lon'), may hold values from -6 to 6
- random_fields: bfloat16 [4, 16, 128, 512], P('ens', None, 'lat', 'lon'), may hold values from -6 to 6
- observed: float32 [6, 13, 128, 512], P(None, None, 'lat', 'lon'), may hold values from -6 to 6
- input_weight: bfloat16 [256, 222], replicated, may hold values from -0.375 to 0.375
- random_weight: bfloat16 [256, 16], replicated, may hold values from -1.5 to 1.5
- hidden_weight: bfloat16 [256, 256], replicated, may hold values from -0.375 to 0.375
- output_weight: bfloat16 [222, 256], replicated, may hold values from -0.375 to 0.375
- diffusivity: float32 [222], replicated, may hold values from 0.02 to 0.24
Outputs:
- grad_state: bfloat16 [4, 222, 128, 512], P('ens', None, 'lat', 'lon')
- grad_w_in: float32 [256, 222], replicated
- grad_w_noise: float32 [256, 16], replicated
- grad_w_mid: float32 [256, 256], replicated
- grad_w_out: float32 [222, 256], replicated
- grad_diffusivity: float32 [222], replicated
All inputs are finite; a program needn't handle non-finite values.
Results may differ from a plain program's by a relative error of at most 0.008.
Values may be sent and summed in bfloat16 or wider, within the bound.
No kernel may reach another device: no remote copies, remote signals or barrier semaphores. Data moves between devices by JAX's collectives and lax.ppermute only.
A program may use at most 128 MiB of HBM per device.

v0:
```python
import jax
import jax.numpy as jnp
from jax import lax
from jax.sharding import PartitionSpec as P

PROGNOSTIC_COUNT = 6
LEVEL_COUNT = 37
SCORED = 13
DELTA = 0.1


def with_halo(block, sides, width):
    for axis, dim in sides:
        count = lax.axis_size(axis)
        forward = [(i, i + 1) for i in range(count - 1)]
        forward.append((count - 1, 0))
        backward = [(target, source) for source, target in forward]
        low = lax.ppermute(
            lax.slice_in_dim(block, block.shape[dim] - width, None, axis=dim), axis, forward
        )
        high = lax.ppermute(lax.slice_in_dim(block, 0, width, axis=dim), axis, backward)
        block = jnp.concatenate([low, block, high], axis=dim)
    return block


def softened_slope(diff):
    return diff * lax.rsqrt(diff * diff + DELTA * DELTA)


def silu_slope(value):
    gate = jax.nn.sigmoid(value)
    return gate * (1.0 + value * (1.0 - gate))


def pole_mask(padded):
    lat_id = lax.axis_index("lat")
    lat_count = lax.axis_size("lat")
    row_ids = jnp.arange(padded.shape[2])
    dropped = (row_ids == 0) & (lat_id == 0) | (row_ids == padded.shape[2] - 1) & (
        lat_id == lat_count - 1
    )
    return padded * jnp.logical_not(dropped)[:, None].astype(padded.dtype)


def stencil(padded, field):
    return (
        padded[:, :, 2:, 1:-1]
        + padded[:, :, :-2, 1:-1]
        + padded[:, :, 1:-1, 2:]
        + padded[:, :, 1:-1, :-2]
        - 4.0 * field
    )


def on_device(
    starting_state,
    random_fields,
    observed,
    input_weight,
    random_weight,
    hidden_weight,
    output_weight,
    diffusivity,
):
    resident_members, channels, latitude_rows, longitude_columns = starting_state.shape
    cells = latitude_rows * longitude_columns
    hidden_width = hidden_weight.shape[0]
    evaluated_rows = PROGNOSTIC_COUNT * SCORED
    padded_state = pole_mask(with_halo(starting_state, (("lat", 2), ("lon", 3)), 1))
    start = starting_state.astype(jnp.float32)
    laplacian_initial = stencil(padded_state.astype(jnp.float32), start)
    stepped = start + diffusivity[None, :, None, None] * laplacian_initial
    advanced_partner = stepped.astype(jnp.bfloat16).reshape(resident_members, channels, cells)
    random_flattened = random_fields.reshape(resident_members, random_fields.shape[1], cells)
    first_preactivation = jnp.einsum(
        "hc,mcn->mhn", input_weight, advanced_partner, preferred_element_type=jnp.float32
    )
    first_preactivation = first_preactivation + jnp.einsum(
        "hk,mkn->mhn", random_weight, random_flattened, preferred_element_type=jnp.float32
    )
    first_activation = jax.nn.silu(first_preactivation).astype(jnp.bfloat16)
    second_preactivation = jnp.einsum(
        "hk,mkn->mhn", hidden_weight, first_activation, preferred_element_type=jnp.float32
    )
    second_activation = jax.nn.silu(second_preactivation).astype(jnp.bfloat16)
    w_out_scored = output_weight.reshape(PROGNOSTIC_COUNT, LEVEL_COUNT, hidden_width)[
        :, ::3
    ].reshape(evaluated_rows, hidden_width)
    advanced_evaluated = stepped.reshape(resident_members, PROGNOSTIC_COUNT, LEVEL_COUNT, cells)[
        :, :, ::3
    ].reshape(resident_members, evaluated_rows, cells)
    member_prediction = advanced_evaluated + jnp.einsum(
        "ch,mhn->mcn", w_out_scored, second_activation, preferred_element_type=jnp.float32
    )
    member_prediction = member_prediction.astype(jnp.bfloat16).reshape(
        resident_members, evaluated_rows, latitude_rows, longitude_columns
    )
    observed_target = observed.reshape(evaluated_rows, latitude_rows, longitude_columns)
    own_values = member_prediction.astype(jnp.float32)
    shard_values = lax.all_gather(member_prediction, "ens", axis=0, tiled=True).astype(jnp.float32)

    def accumulate_member(member_index, running):
        partner_member = lax.dynamic_index_in_dim(shard_values, member_index, 0, keepdims=False)
        return running + softened_slope(own_values - partner_member)

    pairwise_sum = lax.fori_loop(
        0, shard_values.shape[0], accumulate_member, jnp.zeros_like(own_values)
    )
    member_count = resident_members * lax.axis_size("ens")
    score_gradient = (
        softened_slope(own_values - observed_target[None]) - pairwise_sum / (member_count - 1.0)
    ).astype(jnp.bfloat16)
    grad_flat = score_gradient.reshape(resident_members, evaluated_rows, cells)
    out_term = jnp.einsum(
        "mcn,mhn->ch", grad_flat, second_activation, preferred_element_type=jnp.float32
    )
    back_second = jnp.einsum(
        "ch,mcn->mhn", w_out_scored, grad_flat, preferred_element_type=jnp.float32
    )
    delta_second = (back_second * silu_slope(second_preactivation)).astype(jnp.bfloat16)
    mid_term = jnp.einsum(
        "mhn,mkn->hk", delta_second, first_activation, preferred_element_type=jnp.float32
    )
    back_first = jnp.einsum(
        "hk,mhn->mkn", hidden_weight, delta_second, preferred_element_type=jnp.float32
    )
    delta_first = (back_first * silu_slope(first_preactivation)).astype(jnp.bfloat16)
    in_term = jnp.einsum(
        "mhn,mcn->hc", delta_first, advanced_partner, preferred_element_type=jnp.float32
    )
    noise_term = jnp.einsum(
        "mhn,mkn->hk", delta_first, random_flattened, preferred_element_type=jnp.float32
    )
    grad_stepped = jnp.einsum(
        "hc,mhn->mcn", input_weight, delta_first, preferred_element_type=jnp.float32
    )
    grad_stepped = (
        grad_stepped.reshape(resident_members, PROGNOSTIC_COUNT, LEVEL_COUNT, cells)
        .at[:, :, ::3]
        .add(
            grad_flat.astype(jnp.float32).reshape(resident_members, PROGNOSTIC_COUNT, SCORED, cells)
        )
    )
    grad_stepped = grad_stepped.reshape(
        resident_members, channels, latitude_rows, longitude_columns
    )
    diffusivity_term = jnp.sum(grad_stepped * laplacian_initial, axis=(0, 2, 3))
    in_term, noise_term, mid_term, out_term, diffusivity_term = lax.psum(
        (in_term, noise_term, mid_term, out_term, diffusivity_term), ("ens", "lat", "lon")
    )
    padded_grad = pole_mask(
        with_halo(grad_stepped.astype(jnp.bfloat16), (("lat", 2), ("lon", 3)), 1).astype(
            grad_stepped.dtype
        )
    )
    grad_laplace = stencil(padded_grad, grad_stepped)
    grad_state = (grad_stepped + diffusivity[None, :, None, None] * grad_laplace).astype(
        jnp.bfloat16
    )
    inverse_count = 1.0 / (
        resident_members
        * lax.axis_size("ens")
        * latitude_rows
        * lax.axis_size("lat")
        * longitude_columns
        * lax.axis_size("lon")
    )
    grad_w_out = (
        jnp.zeros((PROGNOSTIC_COUNT, LEVEL_COUNT, hidden_width), jnp.float32)
        .at[:, ::3]
        .set(out_term.reshape(PROGNOSTIC_COUNT, SCORED, hidden_width))
        .reshape(channels, hidden_width)
    )
    return (
        grad_state,
        in_term * inverse_count,
        noise_term * inverse_count,
        mid_term * inverse_count,
        grad_w_out * inverse_count,
        diffusivity_term * inverse_count,
    )


def solution(mesh):
    in_specs = (
        P("ens", None, "lat", "lon"),
        P("ens", None, "lat", "lon"),
        P(None, None, "lat", "lon"),
        P(),
        P(),
        P(),
        P(),
        P(),
    )
    out_specs = (P("ens", None, "lat", "lon"), P(), P(), P(), P(), P())
    return jax.shard_map(
        on_device, mesh=mesh, in_specs=in_specs, out_specs=out_specs, check_vma=False
    )
```

profile of v0, /device:TPU:0, one launch (start us, length us, event | category | flops | bytes accessed | tf_op | source)
XLA Modules:
  0.0 457.5 jit_solution(17218860512130126049)
XLA Ops:
  7.2 1.9 fusion.34
  9.7 2.0 collective-permute-start.1
  11.7 1.1 reshape.82
  12.8 5.2 %fusion.27 = f32[2,4096,256]{2,1,0:T(8,128)} fusion(bf16[2,16,4096]{2,1,0:T(8,128)(2,1)S(1)} %reshape.82, bf16[256,16]{0,1:T(8,128)(2,1)} %param.14), kind=kOutput, calls=%fused_computation.67 | convolution fusion | flops 67108864 | bytes 8658944 | tf_op jit(solution)/shard_map/hk,mkn->mhn/dot_general | solution.py:78
  18.0 8.3 %copy.76 = bf16[2,222,32,128]{1,2,3,0:T(8,128)(2,1)} copy(bf16[2,222,32,128]{3,2,1,0:T(8,128)(2,1)} %param.10) | data formatting | bytes 7274496 | tf_op args[0]
  26.7 0.8 pad_maximum_fusion.5
  27.5 2.4 collective-permute-start.2
  29.9 2.4 collective-permute-start.3
  32.5 1.6 collective-permute-done.2
  34.5 4.8 %fusion.19 = f32[2,222,34,130]{1,2,3,0:T(8,128)S(1)} fusion(bf16[2,222,34,1]{1,2,3,0:T(8,128)(2,1)S(1)} %collective-permute-done.3, bf16[2,222,1,128]{1,2,3,0:T(2,128)(2,1)S(1)} %copy.81, bf16[2,222,32,128]{1,2,3,0:T(8,128)(2,1)} %copy.76, bf16[2,222,1,128]{1,2,3,0:T(2,128)(2,1)S(1)} %copy.79, bf16[2,222,34,1]{1,2,3,0:T(8,128)(2,1)S(1)} %collective-permute-done.2, ...), kind=kLoop, calls=%fused_computation.44 | loop fusion | flops 23549760 | bytes 11774948 | tf_op jit(solution)/shard_map/convert_element_type | solution.py:71
  39.3 11.2 %fusion.31 = (bf16[2,222,32,128]{1,2,3,0:T(8,128)(2,1)}, f32[2,222,32,128]{1,2,3,0:T(8,128)}, f32[2,222,32,128]{1,2,3,0:T(8,128)}) fusion(f32[222]{0:T(256)S(1)} %copy-done.10, bf16[2,222,32,128]{1,2,3,0:T(8,128)(2,1)} %copy.76, f32[2,222,34,130]{1,2,3,0:T(8,128)S(1)} %fusion.19), kind=kLoop, calls=%fused_computation.75 | loop fusion | flops 16367616 | bytes 50922360 | tf_op jit(solution)/shard_map/convert_element_type | solution.py:73
  50.5 8.3 %copy.83 = bf16[2,222,32,128]{3,2,1,0:T(8,128)(2,1)} copy(bf16[2,222,32,128]{1,2,3,0:T(8,128)(2,1)} %get-tuple-element.126) | data formatting | bytes 7274496 | tf_op jit(solution)/shard_map/convert_element_type | solution.py:73
  58.8 4.4 reshape.81
  63.2 10.1 %copy.82 = f32[2,222,32,128]{3,2,0,1:T(8,128)} copy(f32[2,222,32,128]{1,2,3,0:T(8,128)} %get-tuple-element.127) | data formatting | bytes 14548992 | tf_op jit(solution)/shard_map/add | solution.py:72
  73.3 10.0 %reshape.79 = f32[2,6,37,4096]{3,0,2,1:T(2,128)} reshape(f32[2,222,32,128]{3,2,0,1:T(8,128)} %copy.82) | data formatting | bytes 14548992 | tf_op jit(solution)/shard_map/reshape | solution.py:89
  83.3 2.0 slice.62
  85.4 9.0 %fusion.16 = (bf16[2,256,4096]{1,2,0:T(8,128)(2,1)S(1)}, f32[2,4096,256]{2,1,0:T(8,128)}) fusion(f32[2,4096,256]{2,1,0:T(8,128)} %fusion.27, bf16[2,222,4096]{2,1,0:T(8,128)(2,1)} %reshape.81, bf16[256,222]{0,1:T(8,128)(2,1)S(1)} %copy-done.8), kind=kOutput, calls=%fused_computation.37 | convolution fusion | flops 943718400 | bytes 24722432 | tf_op jit(solution)/shard_map/hc,mcn->mhn/dot_general | solution.py:75
  94.4 4.7 %fusion.10 = (bf16[2,256,4096]{1,2,0:T(8,128)(2,1)S(1)}, f32[2,4096,256]{2,1,0:T(8,128)}) fusion(bf16[2,256,4096]{1,2,0:T(8,128)(2,1)S(1)} %get-tuple-element.139, bf16[256,256]{1,0:T(8,128)(2,1)S(1)} %copy-done), kind=kOutput, calls=%fused_computation.28 | convolution fusion | flops 1084227584 | bytes 16908288 | tf_op jit(solution)/shard_map/hk,mkn->mhn/dot_general | solution.py:82
  99.1 2.0 copy-done.3
  101.1 2.0 fusion.21
  103.1 1.6 reshape.85
  105.3 3.2 convert_element_type.74
  108.5 36.1 %all-gather.2.cloned.1.call-done = bf16[4,78,32,128]{3,2,1,0:T(8,128)(2,1)} async-done(((bf16[2,78,32,128]{3,2,1,0:T(8,128)(2,1)}), bf16[4,78,32,128]{3,2,1,0:T(8,128)(2,1)}) %all-gather.2.cloned.1.call-update) | async-done | bytes 2555920 | tf_op jit(solution)/shard_map/all_gather | solution.py:100
  144.6 4.8 %convert_element_type.75 = f32[4,78,32,128]{3,2,1,0:T(8,128)} convert(bf16[4,78,32,128]{3,2,1,0:T(8,128)(2,1)} %all-gather.2.cloned.1.call-done) | non-fusion elementwise | flops 1277952 | bytes 7667712 | tf_op jit(solution)/shard_map/convert_element_type | solution.py:100
  149.4 24.0 %while.14 = (s32[]{:T(128)}, f32[2,78,32,128]{3,2,1,0:T(8,128)}, f32[4,78,32,128]{3,2,1,0:T(8,128)}, f32[2,78,32,128]{3,2,1,0:T(8,128)}, s32[]{:T(128)}, /*index=5*/s32[]{:T(128)}) while((s32[]{:T(128)}, f32[2,78,32,128]{3,2,1,0:T(8,128)}, f32[4,78,32,128]{3,2,1,0:T(8,128)}, f32[2,78,32,128]{3,2,1,0:T(8,128)}, s32[]{:T(128)}, ...), condition=%wide.region_1.2_spmd.clone, body=%wide.region_0.1_spmd.clone.sunk | while | flops 3833859 | bytes 11501651 | solution.py:106
  149.4 1.5 dynamic-slice_bitcast_fusion.2
  150.9 4.0 select_add_fusion.2
  154.9 1.4 dynamic-slice_bitcast_fusion.2
  156.3 4.8 %select_add_fusion.2 = f32[2,78,32,128]{3,2,1,0:T(8,128)} fusion(f32[2,78,32,128]{3,2,1,0:T(8,128)} %get-tuple-element.175, f32[2,78,32,128]{3,2,1,0:T(8,128)} %get-tuple-element.183, f32[78,32,128]{2,1,0:T(8,128)S(1)} %dynamic-slice_bitcast_fusion.2, pred[]{:T(512)S(6)} %compare.3), kind=kLoop, calls=%fused_computation.2.clone.1 | loop fusion | flops 3833856 | bytes 8945665 | tf_op jit(solution)/shard_map/while/body/eval_jaxpr/add | solution.py:104
  161.1 1.4 dynamic-slice_bitcast_fusion.2
  162.5 4.8 %select_add_fusion.2 = f32[2,78,32,128]{3,2,1,0:T(8,128)} fusion(f32[2,78,32,128]{3,2,1,0:T(8,128)} %get-tuple-element.175, f32[2,78,32,128]{3,2,1,0:T(8,128)} %get-tuple-element.183, f32[78,32,128]{2,1,0:T(8,128)S(1)} %dynamic-slice_bitcast_fusion.2, pred[]{:T(512)S(6)} %compare.3), kind=kLoop, calls=%fused_computation.2.clone.1 | loop fusion | flops 3833856 | bytes 8945665 | tf_op jit(solution)/shard_map/while/body/eval_jaxpr/add | solution.py:104
  167.3 1.4 dynamic-slice_bitcast_fusion.2
  168.7 4.8 %select_add_fusion.2 = f32[2,78,32,128]{3,2,1,0:T(8,128)} fusion(f32[2,78,32,128]{3,2,1,0:T(8,128)} %get-tuple-element.175, f32[2,78,32,128]{3,2,1,0:T(8,128)} %get-tuple-element.183, f32[78,32,128]{2,1,0:T(8,128)S(1)} %dynamic-slice_bitcast_fusion.2, pred[]{:T(512)S(6)} %compare.3), kind=kLoop, calls=%fused_computation.2.clone.1 | loop fusion | flops 3833856 | bytes 8945665 | tf_op jit(solution)/shard_map/while/body/eval_jaxpr/add | solution.py:104
  173.4 2.8 subtract_convert_fusion
  177.0 3.2 convolution_bitcast_fusion.4
  180.2 6.4 %fusion.6 = bf16[2,256,4096]{1,2,0:T(8,128)(2,1)S(1)} fusion(f32[2,4096,256]{2,1,0:T(8,128)} %get-tuple-element.142, bf16[2,78,4096]{2,1,0:T(8,128)(2,1)S(1)} %reshape.86, bf16[78,256,1]{1,0,2:T(8,128)(2,1)S(1)} %reshape.110), kind=kOutput, calls=%fused_computation.21 | convolution fusion | flops 346030080 | bytes 13900800 | tf_op jit(solution)/shard_map/ch,mcn->mhn/dot_general | solution.py:117
  186.6 2.0 convolution_bitcast_fusion.2
  188.6 3.5 fusion.5
  192.2 1.8 convolution_bitcast_fusion.3
  194.0 4.4 convolution_bitcast_fusion
  198.4 1.8 copy.88
  200.9 11.8 %copy.87 = f32[2,222,4096]{2,0,1:T(2,128)} copy(f32[2,222,4096]{2,1,0:T(8,128)} %convolution_bitcast_fusion) | data formatting | bytes 14548992 | tf_op jit(solution)/shard_map/hc,mhn->mcn/transpose | solution.py:134
  212.7 2.4 reshape.92
  215.1 1.9 copy.89
  217.0 16.4 %scatter_fusion = f32[2,6,37,4096]{3,0,2,1:T(2,128)} fusion(f32[2,6,37,4096]{3,0,2,1:T(2,128)} %bitcast.129, s32[13]{0:T(128)S(1)} %multiply_bitcast_fusion, f32[13,2,6,4096]{3,1,2,0:T(2,128)S(1)} %copy.89), kind=kCustom, calls=%fused_computation | custom fusion | flops 638976 | bytes 7667764 | tf_op jit(solution)/shard_map/scatter-add | solution.py:140
  233.4 10.9 %reshape.88 = f32[2,222,32,128]{3,2,0,1:T(8,128)} reshape(f32[2,6,37,4096]{3,0,2,1:T(2,128)} %scatter_fusion) | data formatting | bytes 14548992 | tf_op jit(solution)/shard_map/reshape | solution.py:144
  244.3 10.1 %copy.96 = f32[2,222,32,128]{1,2,3,0:T(8,128)} copy(f32[2,222,32,128]{3,2,0,1:T(8,128)} %reshape.88) | data formatting | bytes 14548992 | tf_op jit(solution)/shard_map/reshape | solution.py:144
  254.4 10.2 %multiply_reduce_fusion = (f32[222]{0:T(256)S(1)}, bf16[2,222,32,128]{1,2,3,0:T(8,128)(2,1)S(1)}) fusion(f32[2,222,32,128]{1,2,3,0:T(8,128)} %copy.96, f32[2,222,32,128]{1,2,3,0:T(8,128)} %get-tuple-element.128), kind=kLoop, calls=%fused_computation.40 | loop fusion | flops 5455650 | bytes 18187128 | tf_op jit(solution)/shard_map/reduce_sum | solution.py:147
  264.6 2.0 copy-done.1
  267.4 1.8 collective-permute-start.5
  269.2 39.4 %all-reduce = (f32[256,16]{0,1:T(8,128)S(1)}, f32[222]{0:T(256)S(1)}) all-reduce(f32[256,16]{0,1:T(8,128)S(1)} %convolution_bitcast_fusion.5, f32[222]{0:T(256)S(1)} %get-tuple-element.129), channel_id=1, replica_groups=mesh['ens'=2,'lat'=4,'lon'=4] {'ens','lat','lon'}, use_global_device_ids=true, to_apply=%region_4.5 | all-reduce | flops 4318 | bytes 34544 | tf_op jit(solution)/shard_map/psum | solution.py:148
  309.6 0.8 pad_maximum_fusion.2
  310.5 1.5 collective-permute-start.6
  312.0 2.4 collective-permute-start.7
  314.9 0.7 copy.102
  315.6 0.8 collective-permute-done.6
  316.4 8.6 %convert_multiply_fusion = f32[2,222,34,130]{1,2,3,0:T(8,128)} fusion(bf16[2,222,34,1]{1,2,3,0:T(8,128)(2,1)S(1)} %collective-permute-done.7, bf16[2,222,1,128]{1,2,3,0:T(2,128)(2,1)S(1)} %copy.94, bf16[2,222,32,128]{1,2,3,0:T(8,128)(2,1)} %copy-done.1, bf16[2,222,1,128]{1,2,3,0:T(2,128)(2,1)S(1)} %copy.93, ...), kind=kLoop, calls=%fused_computation.4 | loop fusion | flops 21587280 | bytes 11775016 | tf_op jit(solution)/shard_map/mul | solution.py:42
  325.0 19.3 %fusion.4 = bf16[2,222,32,128]{1,2,3,0:T(8,128)(2,1)} fusion(f32[2,222,32,128]{1,2,3,0:T(8,128)} %copy.96, f32[2,222,34,130]{1,2,3,0:T(8,128)} %convert_multiply_fusion, f32[222]{0:T(256)S(1)} %copy-done.10), kind=kLoop, calls=%fused_computation.12 | loop fusion | flops 14548992 | bytes 40010616 | tf_op jit(solution)/shard_map/convert_element_type | solution.py:157
  344.3 8.3 %copy.105 = bf16[2,222,32,128]{3,2,1,0:T(8,128)(2,1)} copy(bf16[2,222,32,128]{1,2,3,0:T(8,128)(2,1)} %fusion.4) | data formatting | bytes 7274496
  352.6 92.1 %all-reduce.4.cloned.1.call-done = (f32[256,222]{0,1:T(8,128)}, f32[256,256]{1,0:T(8,128)}, f32[6,13,256]{2,0,1:T(8,128)}) async-done(((f32[256,222]{0,1:T(8,128)}, f32[256,256]{1,0:T(8,128)}, f32[6,13,256]{2,0,1:T(8,128)}), (f32[256,222]{0,1:T(8,128)}, f32[256,256]{1,0:T(8,128)}, f32[6,13,256]{2,0,1:T(8,128)})) %all-reduce.4.cloned.1.call-update) | async-done | bytes 569360 | tf_op jit(solution)/shard_map/psum | solution.py:148
  444.7 1.7 scatter_fusion.1
  446.4 0.7 mul.158
  447.2 1.7 broadcast_multiply_fusion
  448.8 1.6 broadcast_multiply_fusion.1
  (60 shorter events, 6.1 us)
Async XLA Ops:
  7.2 87.2 %copy-start = (bf16[256,256]{1,0:T(8,128)(2,1)S(1)}, bf16[256,256]{1,0:T(8,128)(2,1)}, u32[]{:S(2)}) copy-start(bf16[256,256]{1,0:T(8,128)(2,1)} %param.15) | copy-start | bytes 393220
  7.2 137.4 %all-gather.2.cloned.1.call-start = ((), (), s32[]{:S(2)}) async-start(), calls=%async_computation | async-start | bytes 3833856 | tf_op jit(solution)/shard_map/all_gather | solution.py:100
  9.1 17.2 %collective-permute-start = (bf16[2,222,1,128]{3,1,2,0:T(8,128)(2,1)S(1)}, bf16[2,222,1,128]{3,1,2,0:T(8,128)(2,1)S(1)}, u32[]{:S(2)}, u32[]{:S(2)}) collective-permute-start(bf16[2,222,1,128]{3,1,2,0:T(8,128)(2,1)S(1)} %copy.113), channel_id=1, source_target_pairs={{0,4},{4,8},{8,12},{12,0},{1,5},{5,9},{9,13},{13,1},{2,6},{6,10},{... | collective-permute-start | bytes 341000 | tf_op jit(solution)/shard_map/ppermute | solution.py:18
  9.7 16.8 %collective-permute-start.1 = (bf16[2,222,1,128]{3,1,2,0:T(8,128)(2,1)S(1)}, bf16[2,222,1,128]{3,1,2,0:T(8,128)(2,1)S(1)}, u32[]{:S(2)}, u32[]{:S(2)}) collective-permute-start(bf16[2,222,1,128]{3,1,2,0:T(8,128)(2,1)S(1)} %copy.114), channel_id=1, source_target_pairs={{4,0},{8,4},{12,8},{0,12},{5,1},{9,5},{13,9},{1,13},{6,2},{10,6},{... | collective-permute-start | bytes 341000 | tf_op jit(solution)/shard_map/ppermute | solution.py:21
  18.0 14.3 %copy-start.9 = (bf16[222,256]{1,0:T(8,128)(2,1)S(1)}, bf16[222,256]{1,0:T(8,128)(2,1)}, u32[]{:S(2)}) copy-start(bf16[222,256]{1,0:T(8,128)(2,1)} %param.16) | copy-start | bytes 340996
  27.5 6.5 %collective-permute-start.2 = (bf16[2,222,34,1]{1,2,3,0:T(8,128)(2,1)S(1)}, bf16[2,222,34,1]{1,2,3,0:T(8,128)(2,1)S(1)}, u32[]{:S(2)}, u32[]{:S(2)}) collective-permute-start(bf16[2,222,34,1]{1,2,3,0:T(8,128)(2,1)S(1)} %get-tuple-element.133), channel_id=1, source_target_pairs={{0,1},{1,2},{2,3},{3,0},{4,5},{5,6},{6,7},{7,4},{8,9},{9,10},{10,1... | collective-permute-start | bytes 90584 | tf_op jit(solution)/shard_map/ppermute | solution.py:18
  29.9 4.5 collective-permute-start.3
  32.4 6.8 %copy-start.10 = (f32[222]{0:T(256)S(1)}, f32[222]{0:T(256)}, u32[]{:S(2)}) copy-start(f32[222]{0:T(256)} %param.17) | copy-start | bytes 2668
  73.3 12.0 %copy-start.8 = (bf16[256,222]{0,1:T(8,128)(2,1)S(1)}, bf16[256,222]{0,1:T(8,128)(2,1)}, u32[]{:S(2)}) copy-start(bf16[256,222]{0,1:T(8,128)(2,1)} %param.13) | copy-start | bytes 340996
  94.4 4.7 %copy-start.4 = (bf16[2,256,4096]{1,2,0:T(8,128)(2,1)}, bf16[2,256,4096]{1,2,0:T(8,128)(2,1)S(1)}, u32[]{:S(2)}) copy-start(bf16[2,256,4096]{1,2,0:T(8,128)(2,1)S(1)} %get-tuple-element.139) | copy-start | bytes 12582916
  99.1 2.0 copy-start.3
  104.7 339.9 %all-reduce.4.cloned.1.call-start = ((), (), s32[]{:S(2)}) async-start(), calls=%async_computation.1 | async-start | bytes 1196032 | tf_op jit(solution)/shard_map/psum | solution.py:148
  149.4 24.0 %copy-start.2 = (bf16[2,78,32,128]{3,2,1,0:T(8,128)(2,1)S(1)}, bf16[2,78,32,128]{3,2,1,0:T(8,128)(2,1)}, u32[]{:S(2)}) copy-start(bf16[2,78,32,128]{3,2,1,0:T(8,128)(2,1)} %reshape.85) | copy-start | bytes 3833860
  177.0 11.7 %slice-start = ((s8[8388608]{0:T(1024)(128)(4,1)}), s8[4194304]{0:T(1024)(128)(4,1)S(1)}, s32[]{:S(2)}) async-start(s8[8388608]{0:T(1024)(128)(4,1)} %bitcast.134), calls=%async_computation.2 | async-start | bytes 8388608
  180.2 6.5 %copy-start.5 = (bf16[2,256,4096]{1,2,0:T(8,128)(2,1)S(1)}, bf16[2,256,4096]{1,2,0:T(8,128)(2,1)}, u32[]{:S(2)}) copy-start(bf16[2,256,4096]{1,2,0:T(8,128)(2,1)} %copy-done.4) | copy-start | bytes 12582916
  180.2 8.5 %slice-start.1 = ((s8[8388608]{0:T(1024)(128)(4,1)}), s8[4194304]{0:T(1024)(128)(4,1)S(1)}, s32[]{:S(2)}) async-start(s8[8388608]{0:T(1024)(128)(4,1)} %bitcast.134), calls=%async_computation.3 | async-start | bytes 8388608
  188.6 3.6 copy-start.7
  200.9 11.8 %copy-start.6 = (f32[2,78,32,128]{3,2,0,1:T(8,128)S(1)}, f32[2,78,32,128]{3,2,0,1:T(8,128)}, u32[]{:S(2)}) copy-start(f32[2,78,32,128]{3,2,0,1:T(8,128)} %copy.88) | copy-start | bytes 7667716
  264.6 2.0 copy-start.1
  267.2 42.1 %collective-permute-start.4 = (bf16[2,222,1,128]{3,1,2,0:T(8,128)(2,1)S(1)}, bf16[2,222,1,128]{3,1,2,0:T(8,128)(2,1)S(1)}, u32[]{:S(2)}, u32[]{:S(2)}) collective-permute-start(bf16[2,222,1,128]{3,1,2,0:T(8,128)(2,1)S(1)} %copy.91), channel_id=1, source_target_pairs={{0,4},{4,8},{8,12},{12,0},{1,5},{5,9},{9,13},{13,1},{2,6},{6,10},{... | collective-permute-start | bytes 341000 | tf_op jit(solution)/shard_map/ppermute | solution.py:18
  267.4 42.0 %collective-permute-start.5 = (bf16[2,222,1,128]{3,1,2,0:T(8,128)(2,1)S(1)}, bf16[2,222,1,128]{3,1,2,0:T(8,128)(2,1)S(1)}, u32[]{:S(2)}, u32[]{:S(2)}) collective-permute-start(bf16[2,222,1,128]{3,1,2,0:T(8,128)(2,1)S(1)} %copy.92), channel_id=1, source_target_pairs={{4,0},{8,4},{12,8},{0,12},{5,1},{9,5},{13,9},{1,13},{6,2},{10,6},{... | collective-permute-start | bytes 341000 | tf_op jit(solution)/shard_map/ppermute | solution.py:21
  310.5 6.0 %collective-permute-start.6 = (bf16[2,222,34,1]{1,2,3,0:T(8,128)(2,1)S(1)}, bf16[2,222,34,1]{1,2,3,0:T(8,128)(2,1)S(1)}, u32[]{:S(2)}, u32[]{:S(2)}) collective-permute-start(bf16[2,222,34,1]{1,2,3,0:T(8,128)(2,1)S(1)} %get-tuple-element.131), channel_id=1, source_target_pairs={{0,1},{1,2},{2,3},{3,0},{4,5},{5,6},{6,7},{7,4},{8,9},{9,10},{10,1... | collective-permute-start | bytes 90584 | tf_op jit(solution)/shard_map/ppermute | solution.py:18
  312.0 4.4 collective-permute-start.7
Sparse Core Ops, SparseCore 0:
  104.9 39.6 all-gather.1
  315.8 128.8 all-reduce.3
where the time goes:
time: 463 us; the launch traced here: 458 us
  waiting for transfers between devices  131 us (28%)
  local copies, waits for them, and re-layouts  110 us (24%)
  other arithmetic  106 us (23%)
  matrix products  43 us (9%)
  blocking collectives  39.4 us (9%)
  between operations  14.6 us (3%)
  starting transfers between devices  13.7 us (3%)
    psum x1, waiting for transfers between devices, on_device(): lax.psum((in_term, noise_term, mid_term, out_term, diffusivity_term), ('e...  92.1 us
    psum x1, blocking collectives, on_device(): lax.psum((in_term, noise_term, mid_term, out_term, diffusivity_term), ('e...  39.4 us
    all_gather x1, waiting for transfers between devices, on_device(): lax.all_gather(member_prediction, 'ens', axis=0, tiled=True)  36.1 us
    reshape x2, local copies, waits for them, and re-layouts, on_device(): grad_stepped.reshape(resident_members, channels, latitude_rows, longitude...  20.9 us
    unnamed x30, local copies, waits for them, and re-layouts  20.7 us
    convert_element_type x1, other arithmetic, on_device(): (grad_stepped + diffusivity[None, :, None, None] * grad_laplace).astype(j...  19.3 us
    add x4, other arithmetic, accumulate_member(): return running + softened_slope(own_values - partner_member)  18.3 us
    scatter-add x1, other arithmetic, on_device(): grad_stepped = grad_stepped.reshape(resident_members, PROGNOSTIC_COUNT, L...  16.4 us
  transfers between devices with their start and end apart: 10, of which 5 were waited for; matrix products, arithmetic and copies ran while one was open for 12% of the time, Pallas kernels for 0%

commit v1 on v0

--- a/solution.py
+++ b/solution.py
@@ -7,6 +7,28 @@
 LEVEL_COUNT = 37
 SCORED = 13
 DELTA = 0.1
+
+
+def joined_along(blocks, dim):
+    blocks = jnp.moveaxis(blocks, 0, dim)
+    dims = blocks.shape
+    return blocks.reshape(*dims[:dim], dims[dim] * dims[dim + 1], *dims[dim + 2 :])
+
+
+def collected_by_bits(value, axis):
+    peers = lax.axis_size(axis)
+    blocks = value[None]
+    for level in range(peers.bit_length() - 1):
+        distance = 1 << level
+        other = lax.ppermute(blocks, axis, [(i, i ^ distance) for i in range(peers)])
+        both = jnp.stack([blocks, other])
+        upper = lax.axis_index(axis) >> level & 1
+        blocks = jnp.where(upper == 0, both, both[::-1]).reshape(-1, *value.shape)
+    return blocks
+
+
+def gather_by_bits(x, axis, dim):
+    return joined_along(collected_by_bits(x, axis), dim)
 
 
 def with_halo(block, sides, width):
@@ -97,7 +119,7 @@
     )
     observed_target = observed.reshape(evaluated_rows, latitude_rows, longitude_columns)
     own_values = member_prediction.astype(jnp.float32)
-    shard_values = lax.all_gather(member_prediction, "ens", axis=0, tiled=True).astype(jnp.float32)
+    shard_values = gather_by_bits(member_prediction, "ens", 0).astype(jnp.float32)
 
     def accumulate_member(member_index, running):
         partner_member = lax.dynamic_index_in_dim(shard_values, member_index, 0, keepdims=False)

time: 463 us -> 449 us (0.970)
  other arithmetic: 106 us -> 92.6 us
  local copies, waits for them, and re-layouts: 110 us -> 123 us
  waiting for transfers between devices: 131 us -> 120 us
    all_gather x1 -> x0, waiting for transfers between devices: 36.1 us -> none  [on_device(): lax.all_gather(member_prediction, 'ens', axis=0, tiled=True)]
    ppermute x0 -> x1, waiting for transfers between devices: none -> 24.7 us  [collected_by_bits(): lax.ppermute(blocks, axis, [(i, i ^ distance) for i in range(peers)])]
    add x4, other arithmetic: 18.3 us -> 6.38 us  [accumulate_member(): return running + softened_slope(own_values - partner_member)]
    while x0 -> x16, local copies, waits for them, and re-layouts: none -> 8.08 us
    convert_element_type x2 -> x1, other arithmetic: 7.99 us -> 3.17 us  [on_device(): gather_by_bits(member_prediction, 'ens', 0).astype(jnp.float32)]
    unnamed x30 -> x32, local copies, waits for them, and re-layouts: 20.7 us -> 21.9 us
  transfers between devices with their start and end apart: 10 -> 10, of which waited for: 5 -> 6; matrix products, arithmetic and copies ran while one was open for 12% -> 13% of each run, Pallas kernels for 0% -> 0%
where the time goes in v1:
time: 449 us; the launch traced here: 444 us
  local copies, waits for them, and re-layouts  123 us (27%)
  waiting for transfers between devices  120 us (27%)
  other arithmetic  92.6 us (21%)
  matrix products  41.2 us (9%)
  blocking collectives  40 us (9%)
  between operations  14.6 us (3%)
  starting transfers between devices  12.7 us (3%)
    psum x1, waiting for transfers between devices, on_device(): lax.psum((in_term, noise_term, mid_term, out_term, diffusivity_term), ('e...  91.4 us
    psum x1, blocking collectives, on_device(): lax.psum((in_term, noise_term, mid_term, out_term, diffusivity_term), ('e...  40 us
    ppermute x1, waiting for transfers between devices, collected_by_bits(): lax.ppermute(blocks, axis, [(i, i ^ distance) for i in range(peers)])  24.7 us
    unnamed x32, local copies, waits for them, and re-layouts  21.9 us
    reshape x2, local copies, waits for them, and re-layouts, on_device(): grad_stepped.reshape(resident_members, channels, latitude_rows, longitude...  20.9 us
    convert_element_type x1, other arithmetic, on_device(): (grad_stepped + diffusivity[None, :, None, None] * grad_laplace).astype(j...  19.3 us
    scatter-add x1, other arithmetic, on_device(): grad_stepped = grad_stepped.reshape(resident_members, PROGNOSTIC_COUNT, L...  16.7 us
    transpose x1, local copies, waits for them, and re-layouts, on_device(): jnp.einsum('hc,mhn->mcn', input_weight, delta_first, preferred_element_ty...  11.6 us
  transfers between devices with their start and end apart: 10, of which 6 were waited for; matrix products, arithmetic and copies ran while one was open for 13% of the time, Pallas kernels for 0%

profile of v1, /device:TPU:0, one launch (start us, length us, event | category | flops | bytes accessed | tf_op | source)
XLA Modules:
  0.0 443.7 jit_solution(11544949695103647187)
XLA Ops:
  7.2 1.9 fusion.34
  9.1 2.5 collective-permute-start.1
  12.8 5.2 %fusion.27 = f32[2,4096,256]{2,1,0:T(8,128)} fusion(bf16[2,16,4096]{2,1,0:T(8,128)(2,1)S(1)} %reshape.84, bf16[256,16]{0,1:T(8,128)(2,1)} %param.14), kind=kOutput, calls=%fused_computation.70 | convolution fusion | flops 67108864 | bytes 8658944 | tf_op jit(solution)/shard_map/hk,mkn->mhn/dot_general | solution.py:100
  18.0 8.3 %copy.76 = bf16[2,222,32,128]{1,2,3,0:T(8,128)(2,1)} copy(bf16[2,222,32,128]{3,2,1,0:T(8,128)(2,1)} %param.10) | data formatting | bytes 7274496 | tf_op args[0]
  27.5 1.6 collective-permute-start.2
  29.1 2.5 collective-permute-start.3
  31.8 1.9 collective-permute-done.2
  34.1 4.8 %fusion.19 = f32[2,222,34,130]{1,2,3,0:T(8,128)S(1)} fusion(bf16[2,222,34,1]{1,2,3,0:T(8,128)(2,1)S(1)} %collective-permute-done.3, bf16[2,222,1,128]{1,2,3,0:T(2,128)(2,1)S(1)} %copy.81, bf16[2,222,32,128]{1,2,3,0:T(8,128)(2,1)} %copy.76, bf16[2,222,1,128]{1,2,3,0:T(2,128)(2,1)S(1)} %copy.79, bf16[2,222,34,1]{1,2,3,0:T(8,128)(2,1)S(1)} %collective-permute-done.2, ...), kind=kLoop, calls=%fused_computation.44 | loop fusion | flops 23549760 | bytes 11774948 | tf_op jit(solution)/shard_map/convert_element_type | solution.py:93
  39.0 11.2 %fusion.31 = (bf16[2,222,32,128]{1,2,3,0:T(8,128)(2,1)}, f32[2,222,32,128]{1,2,3,0:T(8,128)}, f32[2,222,32,128]{1,2,3,0:T(8,128)}) fusion(f32[222]{0:T(256)S(1)} %copy-done.13, bf16[2,222,32,128]{1,2,3,0:T(8,128)(2,1)} %copy.76, f32[2,222,34,130]{1,2,3,0:T(8,128)S(1)} %fusion.19), kind=kLoop, calls=%fused_computation.78 | loop fusion | flops 16367616 | bytes 50922360 | tf_op jit(solution)/shard_map/convert_element_type | solution.py:95
  50.1 8.3 %copy.83 = bf16[2,222,32,128]{3,2,1,0:T(8,128)(2,1)} copy(bf16[2,222,32,128]{1,2,3,0:T(8,128)(2,1)} %get-tuple-element.126) | data formatting | bytes 7274496 | tf_op jit(solution)/shard_map/convert_element_type | solution.py:95
  58.4 4.3 reshape.83
  62.7 10.1 %copy.82 = f32[2,222,32,128]{3,2,0,1:T(8,128)} copy(f32[2,222,32,128]{1,2,3,0:T(8,128)} %get-tuple-element.127) | data formatting | bytes 14548992 | tf_op jit(solution)/shard_map/add | solution.py:94
  72.8 9.9 %reshape.81 = f32[2,6,37,4096]{3,0,2,1:T(2,128)} reshape(f32[2,222,32,128]{3,2,0,1:T(8,128)} %copy.82) | data formatting | bytes 14548992 | tf_op jit(solution)/shard_map/reshape | solution.py:111
  82.8 2.2 slice.62
  85.6 7.3 %fusion.16 = (bf16[2,256,4096]{1,2,0:T(8,128)(2,1)S(1)}, f32[2,4096,256]{2,1,0:T(8,128)}) fusion(f32[2,4096,256]{2,1,0:T(8,128)} %fusion.27, bf16[2,222,4096]{2,1,0:T(8,128)(2,1)S(1)} %copy-done.9, bf16[256,222]{0,1:T(8,128)(2,1)S(1)} %copy-done.11), kind=kOutput, calls=%fused_computation.37 | convolution fusion | flops 943718400 | bytes 24722432 | tf_op jit(solution)/shard_map/hc,mcn->mhn/dot_general | solution.py:97
  93.0 4.6 %fusion.10 = (bf16[2,256,4096]{1,2,0:T(8,128)(2,1)S(1)}, f32[2,4096,256]{2,1,0:T(8,128)}) fusion(bf16[2,256,4096]{1,2,0:T(8,128)(2,1)S(1)} %get-tuple-element.139, bf16[256,256]{1,0:T(8,128)(2,1)S(1)} %copy-done), kind=kOutput, calls=%fused_computation.28 | convolution fusion | flops 1084227584 | bytes 16908288 | tf_op jit(solution)/shard_map/hk,mkn->mhn/dot_general | solution.py:104
  97.6 2.0 copy-done.5
  99.6 2.0 fusion.21
  101.6 1.6 broadcast_in_dim_reshape.4
  103.2 1.5 collective-permute-start.4
  104.7 1.6 stack_broadcast_in_dim_reshape.3
  106.3 2.3 reshape.91
  108.5 24.7 %collective-permute-done.4 = bf16[1,2,78,32,128]{4,3,2,1,0:T(8,128)(2,1)} collective-permute-done((bf16[1,2,78,32,128]{4,3,2,1,0:T(8,128)(2,1)}, bf16[1,2,78,32,128]{4,3,2,1,0:T(8,128)(2,1)}, u32[]{:S(2)}, u32[]{:S(2)}) %collective-permute-start.4) | collective-permute-done | bytes 1277984 | tf_op jit(solution)/shard_map/ppermute | solution.py:23
  133.2 1.9 pad_maximum_fusion
  135.7 3.2 bitcast_convert_fusion
  138.8 20.7 %while.14 = (s32[]{:T(128)}, f32[2,78,32,128]{3,2,1,0:T(8,128)}, f32[4,78,32,128]{3,2,1,0:T(8,128)}, f32[2,78,32,128]{3,2,1,0:T(8,128)S(1)}, s32[]{:T(128)}, /*index=5*/s32[]{:T(128)}) while((s32[]{:T(128)}, f32[2,78,32,128]{3,2,1,0:T(8,128)}, f32[4,78,32,128]{3,2,1,0:T(8,128)}, f32[2,78,32,128]{3,2,1,0:T(8,128)S(1)}, s32[]{:T(128)}, ...), condition=%wide.region_1.2_spmd.clone, body=%wide.region_0.1_spmd.clone.sunk | while | flops 3833859 | bytes 31948948 | solution.py:128
  138.8 1.5 dynamic-slice_bitcast_fusion.2
  140.9 1.6 select_add_fusion.2
  142.5 1.5 copy-done.2
  144.0 1.5 dynamic-slice_bitcast_fusion.2
  146.1 1.6 select_add_fusion.2
  147.7 1.5 copy-done.2
  149.2 1.5 dynamic-slice_bitcast_fusion.2
  151.3 1.6 select_add_fusion.2
  152.9 1.5 copy-done.2
  154.4 1.5 dynamic-slice_bitcast_fusion.2
  156.5 1.6 select_add_fusion.2
  158.1 1.5 copy-done.2
  159.5 3.9 subtract_convert_fusion
  163.5 1.8 reshape.87
  165.2 3.2 convolution_bitcast_fusion.4
  168.4 6.4 %fusion.6 = bf16[2,256,4096]{1,2,0:T(8,128)(2,1)S(1)} fusion(f32[2,4096,256]{2,1,0:T(8,128)} %get-tuple-element.142, bf16[2,78,4096]{2,1,0:T(8,128)(2,1)S(1)} %reshape.87, bf16[78,256,1]{1,0,2:T(8,128)(2,1)S(1)} %reshape.113), kind=kOutput, calls=%fused_computation.21 | convolution fusion | flops 346030080 | bytes 13900800 | tf_op jit(solution)/shard_map/ch,mcn->mhn/dot_general | solution.py:139
  174.9 2.0 convolution_bitcast_fusion.2
  176.9 3.5 fusion.5
  180.5 1.8 convolution_bitcast_fusion.3
  183.9 4.4 convolution_bitcast_fusion
  188.4 2.4 reshape.95
  190.8 1.9 copy.89
  192.7 11.6 %copy.87 = f32[2,222,4096]{2,0,1:T(2,128)} copy(f32[2,222,4096]{2,1,0:T(8,128)} %convolution_bitcast_fusion) | data formatting | bytes 14548992 | tf_op jit(solution)/shard_map/hc,mhn->mcn/transpose | solution.py:156
  204.3 16.7 %scatter_fusion = f32[2,6,37,4096]{3,0,2,1:T(2,128)} fusion(f32[2,6,37,4096]{3,0,2,1:T(2,128)} %bitcast.134, s32[13]{0:T(128)S(1)} %multiply_bitcast_fusion, f32[13,2,6,4096]{3,1,2,0:T(2,128)S(1)} %copy.89), kind=kCustom, calls=%fused_computation | custom fusion | flops 638976 | bytes 7667764 | tf_op jit(solution)/shard_map/scatter-add | solution.py:162
  221.0 10.8 %reshape.89 = f32[2,222,32,128]{3,2,0,1:T(8,128)} reshape(f32[2,6,37,4096]{3,0,2,1:T(2,128)} %scatter_fusion) | data formatting | bytes 14548992 | tf_op jit(solution)/shard_map/reshape | solution.py:166
  231.9 10.1 %copy.96 = f32[2,222,32,128]{1,2,3,0:T(8,128)} copy(f32[2,222,32,128]{3,2,0,1:T(8,128)} %reshape.89) | data formatting | bytes 14548992 | tf_op jit(solution)/shard_map/reshape | solution.py:166
  241.9 9.9 %multiply_reduce_fusion = (f32[222]{0:T(256)S(1)}, bf16[2,222,32,128]{1,2,3,0:T(8,128)(2,1)S(1)}) fusion(f32[2,222,32,128]{1,2,3,0:T(8,128)} %copy.96, f32[2,222,32,128]{1,2,3,0:T(8,128)} %get-tuple-element.128), kind=kLoop, calls=%fused_computation.40 | loop fusion | flops 5455650 | bytes 18187128 | tf_op jit(solution)/shard_map/reduce_sum | solution.py:169
  251.9 2.0 copy-done.3
  255.2 40.0 %all-reduce = (f32[256,16]{0,1:T(8,128)S(1)}, f32[222]{0:T(256)S(1)}) all-reduce(f32[256,16]{0,1:T(8,128)S(1)} %convolution_bitcast_fusion.5, f32[222]{0:T(256)S(1)} %get-tuple-element.129), channel_id=1, replica_groups=mesh['ens'=2,'lat'=4,'lon'=4] {'ens','lat','lon'}, use_global_device_ids=true, to_apply=%region_4.5 | all-reduce | flops 4318 | bytes 34544 | tf_op jit(solution)/shard_map/psum | solution.py:170
  297.0 2.2 collective-permute-start.7
  299.2 1.7 collective-permute-start.8
  303.3 8.6 %convert_multiply_fusion = f32[2,222,34,130]{1,2,3,0:T(8,128)} fusion(bf16[2,222,34,1]{1,2,3,0:T(8,128)(2,1)S(1)} %collective-permute-done.8, bf16[2,222,1,128]{1,2,3,0:T(2,128)(2,1)S(1)} %copy.94, bf16[2,222,32,128]{1,2,3,0:T(8,128)(2,1)} %copy-done.3, bf16[2,222,1,128]{1,2,3,0:T(2,128)(2,1)S(1)} %copy.93, ...), kind=kLoop, calls=%fused_computation.4 | loop fusion | flops 21587280 | bytes 11775016 | tf_op jit(solution)/shard_map/mul | solution.py:64
  311.9 19.3 %fusion.4 = bf16[2,222,32,128]{1,2,3,0:T(8,128)(2,1)} fusion(f32[2,222,32,128]{1,2,3,0:T(8,128)} %copy.96, f32[2,222,34,130]{1,2,3,0:T(8,128)} %convert_multiply_fusion, f32[222]{0:T(256)S(1)} %copy-done.13), kind=kLoop, calls=%fused_computation.12 | loop fusion | flops 14548992 | bytes 40010616 | tf_op jit(solution)/shard_map/convert_element_type | solution.py:179
  331.1 8.3 %copy.105 = bf16[2,222,32,128]{3,2,1,0:T(8,128)(2,1)} copy(bf16[2,222,32,128]{1,2,3,0:T(8,128)(2,1)} %fusion.4) | data formatting | bytes 7274496
  339.4 91.4 %all-reduce.4.cloned.1.call-done = (f32[256,222]{0,1:T(8,128)}, f32[256,256]{1,0:T(8,128)}, f32[6,13,256]{2,0,1:T(8,128)}) async-done(((f32[256,222]{0,1:T(8,128)}, f32[256,256]{1,0:T(8,128)}, f32[6,13,256]{2,0,1:T(8,128)}), (f32[256,222]{0,1:T(8,128)}, f32[256,256]{1,0:T(8,128)}, f32[6,13,256]{2,0,1:T(8,128)})) %all-reduce.4.cloned.1.call-update) | async-done | bytes 569360 | tf_op jit(solution)/shard_map/psum | solution.py:170
  430.9 1.7 scatter_fusion.1
  433.3 1.6 broadcast_multiply_fusion.1
  435.0 1.7 broadcast_multiply_fusion
  (80 shorter events, 14.4 us)
Async XLA Ops:
  7.2 85.8 %copy-start = (bf16[256,256]{1,0:T(8,128)(2,1)S(1)}, bf16[256,256]{1,0:T(8,128)(2,1)}, u32[]{:S(2)}) copy-start(bf16[256,256]{1,0:T(8,128)(2,1)} %param.15) | copy-start | bytes 393220
  7.2 423.7 %all-reduce.4.cloned.1.call-start = ((), (), s32[]{:S(2)}) async-start(), calls=%async_computation | async-start | bytes 1196032 | tf_op jit(solution)/shard_map/psum | solution.py:170
  9.1 17.4 %collective-permute-start.1 = (bf16[2,222,1,128]{3,1,2,0:T(8,128)(2,1)S(1)}, bf16[2,222,1,128]{3,1,2,0:T(8,128)(2,1)S(1)}, u32[]{:S(2)}, u32[]{:S(2)}) collective-permute-start(bf16[2,222,1,128]{3,1,2,0:T(8,128)(2,1)S(1)} %copy.114), channel_id=1, source_target_pairs={{4,0},{8,4},{12,8},{0,12},{5,1},{9,5},{13,9},{1,13},{6,2},{10,6},{... | collective-permute-start | bytes 341000 | tf_op jit(solution)/shard_map/ppermute | solution.py:43
  11.6 14.6 %collective-permute-start = (bf16[2,222,1,128]{3,1,2,0:T(8,128)(2,1)S(1)}, bf16[2,222,1,128]{3,1,2,0:T(8,128)(2,1)S(1)}, u32[]{:S(2)}, u32[]{:S(2)}) collective-permute-start(bf16[2,222,1,128]{3,1,2,0:T(8,128)(2,1)S(1)} %copy.113), channel_id=1, source_target_pairs={{0,4},{4,8},{8,12},{12,0},{1,5},{5,9},{9,13},{13,1},{2,6},{6,10},{... | collective-permute-start | bytes 341000 | tf_op jit(solution)/shard_map/ppermute | solution.py:40
  26.3 5.4 %copy-start.12 = (bf16[222,256]{1,0:T(8,128)(2,1)S(1)}, bf16[222,256]{1,0:T(8,128)(2,1)}, u32[]{:S(2)}) copy-start(bf16[222,256]{1,0:T(8,128)(2,1)} %param.16) | copy-start | bytes 340996
  27.5 6.2 %collective-permute-start.2 = (bf16[2,222,34,1]{1,2,3,0:T(8,128)(2,1)S(1)}, bf16[2,222,34,1]{1,2,3,0:T(8,128)(2,1)S(1)}, u32[]{:S(2)}, u32[]{:S(2)}) collective-permute-start(bf16[2,222,34,1]{1,2,3,0:T(8,128)(2,1)S(1)} %get-tuple-element.133), channel_id=1, source_target_pairs={{0,1},{1,2},{2,3},{3,0},{4,5},{5,6},{6,7},{7,4},{8,9},{9,10},{10,1... | collective-permute-start | bytes 90584 | tf_op jit(solution)/shard_map/ppermute | solution.py:40
  29.1 5.0 %collective-permute-start.3 = (bf16[2,222,34,1]{1,2,3,0:T(8,128)(2,1)S(1)}, bf16[2,222,34,1]{1,2,3,0:T(8,128)(2,1)S(1)}, u32[]{:S(2)}, u32[]{:S(2)}) collective-permute-start(bf16[2,222,34,1]{1,2,3,0:T(8,128)(2,1)S(1)} %get-tuple-element.134), channel_id=1, source_target_pairs={{1,0},{2,1},{3,2},{0,3},{5,4},{6,5},{7,6},{4,7},{9,8},{10,9},{11,1... | collective-permute-start | bytes 90584 | tf_op jit(solution)/shard_map/ppermute | solution.py:43
  31.8 7.2 %copy-start.13 = (f32[222]{0:T(256)S(1)}, f32[222]{0:T(256)}, u32[]{:S(2)}) copy-start(f32[222]{0:T(256)} %param.17) | copy-start | bytes 2668
  82.8 2.8 copy-start.9
  82.8 2.8 copy-start.11
  93.0 4.6 %copy-start.6 = (bf16[2,256,4096]{1,2,0:T(8,128)(2,1)}, bf16[2,256,4096]{1,2,0:T(8,128)(2,1)S(1)}, u32[]{:S(2)}) copy-start(bf16[2,256,4096]{1,2,0:T(8,128)(2,1)S(1)} %get-tuple-element.139) | copy-start | bytes 12582916
  97.6 2.0 copy-start.5
  101.6 3.1 copy-start.4
  103.2 30.0 %collective-permute-start.4 = (bf16[1,2,78,32,128]{4,3,2,1,0:T(8,128)(2,1)}, bf16[1,2,78,32,128]{4,3,2,1,0:T(8,128)(2,1)}, u32[]{:S(2)}, u32[]{:S(2)}) collective-permute-start(bf16[1,2,78,32,128]{4,3,2,1,0:T(8,128)(2,1)} %broadcast_in_dim_reshape.4), channel_id=1, source_target_pairs={{0,16},{16,0},{1,17},{17,1},{2,18},{18,2},{3,19},{19,3},{4,20},{20... | collective-permute-start | bytes 3833864 | tf_op jit(solution)/shard_map/ppermute | solution.py:23
  138.8 2.1 copy-start.1
  142.5 1.5 copy-start.2
  144.0 2.1 copy-start.1
  147.7 1.5 copy-start.2
  149.2 2.1 copy-start.1
  152.9 1.5 copy-start.2
  154.4 2.1 copy-start.1
  158.1 1.5 copy-start.2
  165.2 11.7 %slice-start = ((s8[8388608]{0:T(1024)(128)(4,1)}), s8[4194304]{0:T(1024)(128)(4,1)S(1)}, s32[]{:S(2)}) async-start(s8[8388608]{0:T(1024)(128)(4,1)} %bitcast.139), calls=%async_computation.1 | async-start | bytes 8388608
  168.4 6.5 %copy-start.7 = (bf16[2,256,4096]{1,2,0:T(8,128)(2,1)S(1)}, bf16[2,256,4096]{1,2,0:T(8,128)(2,1)}, u32[]{:S(2)}) copy-start(bf16[2,256,4096]{1,2,0:T(8,128)(2,1)} %copy-done.6) | copy-start | bytes 12582916
  168.4 8.5 %slice-start.1 = ((s8[8388608]{0:T(1024)(128)(4,1)}), s8[4194304]{0:T(1024)(128)(4,1)S(1)}, s32[]{:S(2)}) async-start(s8[8388608]{0:T(1024)(128)(4,1)} %bitcast.139), calls=%async_computation.2 | async-start | bytes 8388608
  176.9 3.6 copy-start.10
  182.3 1.3 copy-start.8
  251.9 2.0 copy-start.3
  254.6 41.4 %collective-permute-start.6 = (bf16[2,222,1,128]{3,1,2,0:T(8,128)(2,1)S(1)}, bf16[2,222,1,128]{3,1,2,0:T(8,128)(2,1)S(1)}, u32[]{:S(2)}, u32[]{:S(2)}) collective-permute-start(bf16[2,222,1,128]{3,1,2,0:T(8,128)(2,1)S(1)} %copy.92), channel_id=1, source_target_pairs={{4,0},{8,4},{12,8},{0,12},{5,1},{9,5},{13,9},{1,13},{6,2},{10,6},{... | collective-permute-start | bytes 341000 | tf_op jit(solution)/shard_map/ppermute | solution.py:43
  255.0 40.8 %collective-permute-start.5 = (bf16[2,222,1,128]{3,1,2,0:T(8,128)(2,1)S(1)}, bf16[2,222,1,128]{3,1,2,0:T(8,128)(2,1)S(1)}, u32[]{:S(2)}, u32[]{:S(2)}) collective-permute-start(bf16[2,222,1,128]{3,1,2,0:T(8,128)(2,1)S(1)} %copy.91), channel_id=1, source_target_pairs={{0,4},{4,8},{8,12},{12,0},{1,5},{5,9},{9,13},{13,1},{2,6},{6,10},{... | collective-permute-start | bytes 341000 | tf_op jit(solution)/shard_map/ppermute | solution.py:40
  297.0 5.9 %collective-permute-start.7 = (bf16[2,222,34,1]{1,2,3,0:T(8,128)(2,1)S(1)}, bf16[2,222,34,1]{1,2,3,0:T(8,128)(2,1)S(1)}, u32[]{:S(2)}, u32[]{:S(2)}) collective-permute-start(bf16[2,222,34,1]{1,2,3,0:T(8,128)(2,1)S(1)} %get-tuple-element.131), channel_id=1, source_target_pairs={{0,1},{1,2},{2,3},{3,0},{4,5},{5,6},{6,7},{7,4},{8,9},{9,10},{10,1... | collective-permute-start | bytes 90584 | tf_op jit(solution)/shard_map/ppermute | solution.py:40
  299.2 4.1 collective-permute-start.8
Sparse Core Ops, SparseCore 0:
  302.3 128.4 all-reduce.3
